TPU v7x, 512 devices: a whole 4x8x8 slice. The times are simulated.
512 devices in a mesh: brick: 64 (over z, y), freq: 8 (over x, core).
Axes of the slice: x: 4, y: 8, z: 8, core: 2. Of those that a mesh axis runs over, the one named last changes fastest.
Arguments:
- forward_fields: bfloat16 [8, 64, 2, 512, 1536], P('freq', 'brick'), may hold values from -6 to 6
- adjoint_panels: bfloat16 [8, 16384, 2, 1536], P('freq', 'brick'), may hold values from -6 to 6
- residual_blocks: bfloat16 [8, 64, 8, 3, 64, 128], P('freq', 'brick'), may hold values from -0.0048828125 to 0.0048828125
- residual_columns: int32 [64, 8, 3], P('brick'), may hold values from 0 to 7, as said below
- panel_brick: int32 [16384, 1], P('brick'), may hold values from 0 to 63; in each aligned block of 256 rows (0 to 255, 256 to 511, ...) at most 8 rows name the same one
- panel_receiver: int32 [16384], P('brick'), may hold values from 0 to 511
Outputs:
- gradient: float32 [32768], P(('brick', 'freq'))
Inputs may be any that keep to these rules, and one draw needn't show every extreme that they name: `panel_brick`: the panels of one device lie on any one brick at most 8 times, and on some brick exactly 8 times. `residual_columns`: the 3 receiver blocks of one transmitter block follow one another cyclically modulo 8.
All inputs are finite; a program needn't handle non-finite values.
Results may differ from a plain program's by a relative error of at most 0.0003.
Values may be sent and summed in bfloat16 or wider, within the bound.
A program may use at most 64 MiB of HBM per device.

v0:
```python
import jax
import jax.numpy as jnp
from jax import lax
from jax.sharding import PartitionSpec as P


def pick_columns(blocks, columns, receivers):
    width = blocks.shape[-2]
    rblock = jnp.where(receivers >= 0, receivers // width, -1).astype(jnp.int32)
    offset = (receivers % width).astype(jnp.int32)
    match = (columns[:, :, None] == rblock[None, None, :]).astype(jnp.float32)
    onehot = (jnp.arange(width, dtype=jnp.int32)[:, None] == offset[None, :]).astype(jnp.float32)
    values = blocks.astype(jnp.float32)
    real_part = jnp.einsum(
        "kjto,os->kjts", values[..., :width], onehot, precision=lax.Precision.HIGHEST
    )
    imag_part = jnp.einsum(
        "kjto,os->kjts", values[..., width:], onehot, precision=lax.Precision.HIGHEST
    )
    real_col = jnp.einsum("kjts,kjs->kts", real_part, match, precision=lax.Precision.HIGHEST)
    imag_col = jnp.einsum("kjts,kjs->kts", imag_part, match, precision=lax.Precision.HIGHEST)
    count = real_col.shape[0] * real_col.shape[1]
    real_col = real_col.reshape(count, -1).astype(jnp.bfloat16)
    imag_col = imag_col.reshape(count, -1).astype(jnp.bfloat16)
    return (real_col, imag_col)


def correlate(real_col, imag_col, fields, panels):
    slots = real_col.shape[1]
    left = jnp.concatenate(
        [
            jnp.concatenate([real_col.T, -imag_col.T], axis=1),
            jnp.concatenate([imag_col.T, real_col.T], axis=1),
        ],
        axis=0,
    )
    right = fields.reshape(-1, fields.shape[-1])
    product = jnp.dot(left, right, preferred_element_type=jnp.float32)
    per_panel = product[:slots] * panels[:, 0].astype(jnp.float32) - product[slots:] * panels[
        :, 1
    ].astype(jnp.float32)
    return per_panel.reshape(slots, 3, -1).sum(axis=1)


def on_device(
    forward_fields, adjoint_panels, residual_blocks, residual_columns, panel_brick, panel_receiver
):
    bricks = lax.axis_size("brick")
    held = adjoint_panels.shape[1]
    span = adjoint_panels.shape[3]
    cells = span // 3
    capacity = max(2, 2 * held // bricks)
    target = panel_brick[:, 0]
    member = (target[:, None] == jnp.arange(bricks, dtype=jnp.int32)[None, :]).astype(jnp.int32)
    before = jnp.cumsum(member, axis=0) - member
    place = target * capacity + jnp.sum(before * member, axis=1)
    select = jnp.arange(bricks * capacity, dtype=jnp.int32)[:, None] == place[None, :]
    flat = adjoint_panels[0].reshape(held, 2 * span)
    outgoing = jnp.dot(
        select.astype(jnp.bfloat16), flat, preferred_element_type=jnp.float32
    ).astype(jnp.bfloat16)
    outgoing = outgoing.reshape(bricks, capacity, 2 * span)
    labels = jnp.sum(select.astype(jnp.int32) * (panel_receiver[None, :] + 1), axis=1) - 1
    labels = labels.reshape(bricks, capacity)
    fields = forward_fields[0, 0]
    blocks = residual_blocks[0, 0]
    columns = residual_columns[0]
    buffer, receivers = (
        lax.all_to_all(outgoing, "brick", split_axis=0, concat_axis=0, tiled=True),
        lax.all_to_all(labels, "brick", split_axis=0, concat_axis=0, tiled=True),
    )
    count = buffer.shape[0] * buffer.shape[1]
    panels = buffer.reshape(count, 2, span)
    real_col, imag_col = pick_columns(blocks, columns, receivers.reshape(count))
    terms = correlate(real_col, imag_col, fields, panels)
    local_term = terms.reshape(buffer.shape[0], buffer.shape[1], cells).sum(axis=0).sum(axis=0)
    share = cells // lax.axis_size("freq")
    summed = lax.psum(local_term, "freq")
    return lax.dynamic_slice_in_dim(summed, lax.axis_index("freq") * share, share, 0)


def solution(mesh):
    placed = (
        P("freq", "brick", None, None, None),
        P("freq", "brick", None, None),
        P("freq", "brick", None, None, None, None),
        P("brick", None, None),
        P("brick", None),
        P("brick"),
    )
    return jax.shard_map(
        on_device, mesh=mesh, in_specs=placed, out_specs=P(("brick", "freq")), check_vma=False
    )
```

profile of v0, /device:TPU:112, one launch (start us, length us, event | category | flops | bytes accessed | tf_op | source)
XLA Modules:
  0.0 156.5 jit_solution(11873351922626310613)
XLA Ops:
  0.0 0.0 copy-start
  0.0 0.8 fusion.24
  0.8 0.6 reduce-window.6
  1.4 0.2 slice_reduce_fusion
  1.7 0.8 fusion.21
  2.5 0.7 multiply_add_fusion
  3.2 0.1 select_reduce_fusion
  3.3 0.7 sub.20
  4.0 15.1 %all-to-all-start = ((s32[64,1,8]{2,1,0:T(1,128)}), s32[64,1,8]{2,1,0:T(1,128)S(1)}, u32[]{:S(2)}, u32[]{:S(2)}) async-start(s32[64,1,8]{2,1,0:T(1,128)} %bitcast.8), calls=%async_computation | async-start | bytes 65536 | tf_op jit(solution)/shard_map/all_to_all | solution.py:70
  19.1 1.6 %copy.42 = bf16[32,8,2,1536]{3,1,2,0:T(8,128)(2,1)S(1)} copy(bf16[32,8,2,1536]{3,2,1,0:T(2,128)(2,1)} %bitcast.76) | data formatting | bytes 3145728
  20.8 2.6 %fusion = bf16[64,8,3072]{2,1,0:T(8,128)(2,1)} fusion(bf16[256,3072]{1,0:T(8,128)(2,1)S(1)} %bitcast.75, s32[256]{0:T(256)S(1)} %get-tuple-element.9), kind=kOutput, calls=%fused_computation.1 | convolution fusion | flops 807010304 | bytes 4719616 | tf_op jit(solution)/shard_map/dot_general | solution.py:59
  23.4 0.0 copy-start.2
  23.4 3.8 %all-to-all-done = s32[64,1,8]{2,1,0:T(1,128)S(1)} async-done(((s32[64,1,8]{2,1,0:T(1,128)}), s32[64,1,8]{2,1,0:T(1,128)S(1)}, u32[]{:S(2)}, u32[]{:S(2)}) %all-to-all-start) | async-done | bytes 2080 | tf_op jit(solution)/shard_map/all_to_all | solution.py:70
  27.2 9.4 %all-to-all-start.1 = ((bf16[64,8,3072]{2,1,0:T(8,128)(2,1)}), bf16[64,8,3072]{2,1,0:T(8,128)(2,1)}, u32[]{:S(2)}, u32[]{:S(2)}) async-start(bf16[64,8,3072]{2,1,0:T(8,128)(2,1)} %fusion), calls=%async_computation.1 | async-start | bytes 6291456 | tf_op jit(solution)/shard_map/all_to_all | solution.py:69
  36.7 0.0 copy-done.2
  36.7 0.1 copy.37
  36.8 0.5 broadcast.112
  37.3 0.7 reduce.14
  38.0 0.1 reshape.120
  38.1 0.1 bitcast_convert_fusion
  38.2 1.7 %fusion.3 = bf16[8,512,64]{1,2,0:T(8,128)(2,1)S(1)} fusion(f32[8,512,3]{1,2,0:T(4,128)S(1)} %bitcast_convert_fusion, bf16[8,3,64,128]{3,2,1,0:T(8,128)(2,1)} %bitcast.82, s32[512]{0:T(512)S(1)} %get-tuple-element.7), kind=kOutput, calls=%fused_computation.7 | convolution fusion | flops 102006784 | bytes 968704 | tf_op jit(solution)/shard_map/kjto,os->kjts/dot_general | solution.py:17
  39.9 1.6 %fusion.4 = bf16[8,512,64]{1,2,0:T(8,128)(2,1)S(1)} fusion(f32[8,512,3]{1,2,0:T(4,128)S(1)} %bitcast_convert_fusion, bf16[8,3,64,128]{3,2,1,0:T(8,128)(2,1)} %bitcast.83, s32[512]{0:T(512)S(1)} %get-tuple-element.7), kind=kOutput, calls=%fused_computation.9 | convolution fusion | flops 102006784 | bytes 968704 | tf_op jit(solution)/shard_map/kjto,os->kjts/dot_general | solution.py:14
  41.5 0.1 bitcast_negate_fusion
  41.6 0.0 copy-done
  41.6 12.3 %fusion.5 = f32[1024,1536]{1,0:T(8,128)} fusion(bf16[1024,1536]{1,0:T(8,128)(2,1)S(1)} %bitcast.74, bf16[512,512]{0,1:T(8,128)(2,1)S(1)} %bitcast.84, bf16[512,512]{0,1:T(8,128)(2,1)S(1)} %bitcast.77, bf16[512,512]{0,1:T(8,128)(2,1)S(1)} %bitcast_negate_fusion), kind=kOutput, calls=%fused_computation.10 | convolution fusion | flops 3229614080 | bytes 11010048 | tf_op jit(solution)/shard_map/dot_general | solution.py:38
  53.9 71.2 %all-to-all-done.1 = bf16[64,8,3072]{2,1,0:T(8,128)(2,1)} async-done(((bf16[64,8,3072]{2,1,0:T(8,128)(2,1)}), bf16[64,8,3072]{2,1,0:T(8,128)(2,1)}, u32[]{:S(2)}, u32[]{:S(2)}) %all-to-all-start.1) | async-done | bytes 3145760 | tf_op jit(solution)/shard_map/all_to_all | solution.py:69
  125.1 8.3 %reshape.122 = bf16[512,2,1536]{2,1,0:T(2,128)(2,1)} reshape(bf16[64,8,3072]{2,1,0:T(8,128)(2,1)} %all-to-all-done.1) | data formatting | bytes 6291456 | tf_op jit(solution)/shard_map/reshape | solution.py:73
  133.4 7.7 %fusion.28 = (bf16[512,1,1536]{2,1,0:T(2,128)(2,1)S(1)}, bf16[512,1,1536]{2,1,0:T(2,128)(2,1)S(1)}) fusion(bf16[512,2,1536]{2,1,0:T(2,128)(2,1)} %reshape.122), kind=kLoop, calls=%fused_computation.53 | loop fusion | bytes 6291456 | tf_op jit(solution)/shard_map/slice | solution.py:39
  141.1 0.0 copy-done.1
  141.1 1.5 fusion.2
  142.7 13.2 %psum.7 = f32[512]{0:T(512)S(1)} all-reduce(f32[512]{0:T(512)S(1)} %reduce_sum.46), channel_id=1, replica_groups=mesh['brick'=64,'freq'=8] {'freq'}, use_global_device_ids=true, to_apply=%region_6.7 | all-reduce | flops 512 | bytes 4096 | tf_op jit(solution)/shard_map/psum | solution.py:78
  155.9 0.6 dynamic_slice.3
  (7 shorter events, 0.1 us)
Async XLA Ops:
  0.0 41.6 %copy-start = (bf16[1,1,2,512,1536]{4,3,2,1,0:T(8,128)(2,1)S(1)}, bf16[1,1,2,512,1536]{4,3,2,1,0:T(8,128)(2,1)}, u32[]{:S(2)}) copy-start(bf16[1,1,2,512,1536]{4,3,2,1,0:T(8,128)(2,1)} %param.6) | copy-start | bytes 9437188
  4.0 23.2 %all-to-all-start = ((s32[64,1,8]{2,1,0:T(1,128)}), s32[64,1,8]{2,1,0:T(1,128)S(1)}, u32[]{:S(2)}, u32[]{:S(2)}) async-start(s32[64,1,8]{2,1,0:T(1,128)} %bitcast.8), calls=%async_computation | async-start | bytes 65536 | tf_op jit(solution)/shard_map/all_to_all | solution.py:70
  23.4 13.3 %copy-start.2 = (s32[1,8,3]{1,0,2:T(1,128)S(1)}, s32[1,8,3]{1,0,2:T(1,128)}, u32[]{:S(2)}) copy-start(s32[1,8,3]{1,0,2:T(1,128)} %param.9) | copy-start | bytes 292
  27.2 97.9 %all-to-all-start.1 = ((bf16[64,8,3072]{2,1,0:T(8,128)(2,1)}), bf16[64,8,3072]{2,1,0:T(8,128)(2,1)}, u32[]{:S(2)}, u32[]{:S(2)}) async-start(bf16[64,8,3072]{2,1,0:T(8,128)(2,1)} %fusion), calls=%async_computation.1 | async-start | bytes 6291456 | tf_op jit(solution)/shard_map/all_to_all | solution.py:69
  133.4 7.7 %copy-start.1 = (f32[1024,1536]{1,0:T(8,128)S(1)}, f32[1024,1536]{1,0:T(8,128)}, u32[]{:S(2)}) copy-start(f32[1024,1536]{1,0:T(8,128)} %fusion.5) | copy-start | bytes 18874372
where the time goes:
time: 157 us; the launch traced here: 156 us
  waiting for transfers between devices  75.1 us (48%)
  starting transfers between devices  24.5 us (16%)
  local copies, waits for them, and re-layouts  19.8 us (13%)
  matrix products  18.2 us (12%)
  blocking collectives  13.2 us (8%)
  other arithmetic  5.55 us (4%)
    all_to_all x1, waiting for transfers between devices, on_device(): lax.all_to_all(outgoing, 'brick', split_axis=0, concat_axis=0, tiled=True)  71.2 us
    all_to_all x1, starting transfers between devices, on_device(): lax.all_to_all(labels, 'brick', split_axis=0, concat_axis=0, tiled=True)  15.1 us
    psum x1, blocking collectives, on_device(): summed = lax.psum(local_term, 'freq')  13.2 us
    dot_general x1, matrix products, correlate(): product = jnp.dot(left, right, preferred_element_type=jnp.float32)  12.3 us
    all_to_all x1, starting transfers between devices, on_device(): lax.all_to_all(outgoing, 'brick', split_axis=0, concat_axis=0, tiled=True)  9.44 us
    reshape x1, local copies, waits for them, and re-layouts, on_device(): panels = buffer.reshape(count, 2, span)  8.28 us
    slice x1, local copies, waits for them, and re-layouts, correlate(): panels[:, 0].astype(jnp.float32)  7.71 us
    all_to_all x1, waiting for transfers between devices, on_device(): lax.all_to_all(labels, 'brick', split_axis=0, concat_axis=0, tiled=True)  3.84 us
  transfers between devices with their start and end apart: 2, of which 2 were waited for; matrix products, arithmetic and copies ran while one was open for 14% of the time, Pallas kernels for 0%

commit v1 on v0

v1 whole, which is shorter than its diff:
```python
import functools

import jax
import jax.numpy as jnp
from jax import lax
from jax.experimental import pallas as pl
from jax.experimental.pallas import tpu as pltpu
from jax.sharding import PartitionSpec as P

SIDE = 8
SLOTS = 8
MESH = pl.DeviceIdType.MESH


def zigzag(step):
    half = (step + 1) // 2
    return 4 + half * (1 - 2 * lax.rem(step, 2))


def kernel(
    bricks, freqs, columns_ref, target_ref, receiver_ref, panels_hbm, fields_hbm, blocks_hbm,
    out_ref,
    panels, fields, blocks, outgoing, incoming, labels_out, labels_in, dense, left, product,
    total, partial, gathered,
    load_sem, send_sem, recv_sem, label_send_sem, label_recv_sem, sum_send_sem, sum_recv_sem,
):
    me = lax.axis_index("brick")
    mine = lax.axis_index("freq")
    my_z, my_y = me // SIDE, lax.rem(me, SIDE)
    held, width = panels.shape
    span = fields.shape[1]
    cells = span // 3
    tx = fields.shape[0] // 2

    loads = [
        pltpu.make_async_copy(panels_hbm, panels, load_sem.at[0]),
        pltpu.make_async_copy(blocks_hbm, blocks, load_sem.at[1]),
        pltpu.make_async_copy(fields_hbm, fields, load_sem.at[2]),
    ]
    for load in loads:
        load.start()

    barrier = pltpu.get_barrier_semaphore()

    @pl.loop(1, bricks)
    def _(k):
        pl.semaphore_signal(
            barrier, inc=1, device_id={"brick": lax.rem(me + k, bricks)}, device_id_type=MESH
        )

    @pl.loop(1, freqs)
    def _(k):
        pl.semaphore_signal(
            barrier, inc=1, device_id={"freq": lax.rem(mine + k, freqs)}, device_id_type=MESH
        )

    target = target_ref[...]
    down = lax.broadcasted_iota(jnp.int32, (held, held), 0)
    across = lax.broadcasted_iota(jnp.int32, (held, held), 1)
    diagonal = down == across
    target_col = jnp.sum(jnp.where(diagonal, target, 0), axis=1, keepdims=True)
    same = target_col == target
    rank = jnp.sum(jnp.where(same & (down < across), 1, 0), axis=0, keepdims=True)
    rank_col = jnp.sum(jnp.where(same & (across < down), 1, 0), axis=1, keepdims=True)
    place = target * SLOTS + rank

    value = receiver_ref[...] + 1
    names = lax.broadcasted_iota(jnp.int32, (bricks, held), 0) == target
    lanes = lax.broadcasted_iota(jnp.int32, (held, 128), 1)
    by_rank = (rank_col == lanes).astype(jnp.float32).astype(jnp.bfloat16)
    high = jnp.where(names, value // 16, 0).astype(jnp.float32).astype(jnp.bfloat16)
    low = jnp.where(names, lax.rem(value, 16), 0).astype(jnp.float32).astype(jnp.bfloat16)
    high = jnp.dot(high, by_rank, preferred_element_type=jnp.float32)
    low = jnp.dot(low, by_rank, preferred_element_type=jnp.float32)
    labels_out[...] = (high * 16.0 + low).astype(jnp.int32)

    def label_copy(other, row):
        return pltpu.make_async_remote_copy(
            src_ref=labels_out.at[pl.ds(other, 1)],
            dst_ref=labels_in.at[pl.ds(row, 1)],
            send_sem=label_send_sem.at[other],
            recv_sem=label_recv_sem.at[row],
            device_id={"brick": other},
            device_id_type=MESH,
        )

    def block_copy(other, row):
        return pltpu.make_async_remote_copy(
            src_ref=outgoing.at[other],
            dst_ref=incoming.at[row],
            send_sem=send_sem.at[other],
            recv_sem=recv_sem.at[row],
            device_id={"brick": other},
            device_id_type=MESH,
        )

    def build(z):
        slots = lax.broadcasted_iota(jnp.int32, (SIDE * SLOTS, held), 0) + z * (SIDE * SLOTS)
        select = (slots == place).astype(jnp.float32).astype(jnp.bfloat16)
        rows = jnp.dot(select, panels[...], preferred_element_type=jnp.float32)
        outgoing[pl.ds(z * SIDE, SIDE)] = rows.reshape(SIDE, SLOTS, width).astype(jnp.bfloat16)

    loads[0].wait()
    build(lax.rem(my_z + zigzag(0), SIDE))
    pl.semaphore_wait(barrier, bricks - 1 + freqs - 1)

    @pl.loop(1, bricks)
    def _(k):
        other = lax.rem(me + k, bricks)
        label_copy(other, me).start()

    @pl.loop(0, SIDE)
    def _(step):
        z = lax.rem(my_z + zigzag(step), SIDE)

        @pl.when(step > 0)
        def _():
            build(z)

        @pl.loop(0, SIDE)
        def _(inner):
            y = lax.rem(my_y + zigzag(inner), SIDE)
            other = z * SIDE + y

            @pl.when(other != me)
            def _():
                block_copy(other, me).start()

    loads[1].wait()
    for k in range(columns_ref.shape[0]):
        for r in range(SIDE):
            tile = jnp.zeros((blocks.shape[2], blocks.shape[3]), jnp.bfloat16)
            for j in range(columns_ref.shape[1]):
                tile = jnp.where(columns_ref[k, j] == r, blocks[k, j], tile)
            dense[0, pl.ds(k * 64, 64), pl.ds(r * 64, 64)] = tile[:, :64]
            dense[1, pl.ds(k * 64, 64), pl.ds(r * 64, 64)] = tile[:, 64:]

    labels_in[pl.ds(me, 1)] = labels_out[pl.ds(me, 1)]

    @pl.loop(1, bricks)
    def _(k):
        other = lax.rem(me + k, bricks)
        label_copy(other, other).wait_recv()

    named = labels_in[...]
    pick = lax.broadcasted_iota(jnp.int32, (bricks, SLOTS, 128), 1) == lax.broadcasted_iota(
        jnp.int32, (bricks, SLOTS, 128), 2
    )
    label = jnp.sum(jnp.where(pick, named[:, None, :], 0), axis=2, keepdims=True)
    label = label.reshape(bricks * SLOTS, 1) - 1
    receivers = lax.broadcasted_iota(jnp.int32, (bricks * SLOTS, dense.shape[2]), 1)
    onehot = (receivers == label).astype(jnp.float32).astype(jnp.bfloat16)
    dims = (((1,), (1,)), ((), ()))
    real = lax.dot_general(onehot, dense[0], dims, preferred_element_type=jnp.float32)
    imag = lax.dot_general(onehot, dense[1], dims, preferred_element_type=jnp.float32)
    left[0, :, pl.ds(0, tx)] = real.astype(jnp.bfloat16)
    left[0, :, pl.ds(tx, tx)] = (-imag).astype(jnp.bfloat16)
    left[1, :, pl.ds(0, tx)] = imag.astype(jnp.bfloat16)
    left[1, :, pl.ds(tx, tx)] = real.astype(jnp.bfloat16)

    loads[2].wait()

    @pl.loop(0, 4)
    def _(tile):
        rows = pl.ds(pl.multiple_of(tile * 128, 128), 128)
        product[0, rows] = jnp.dot(left[0, rows], fields[...], preferred_element_type=jnp.float32)
        product[1, rows] = jnp.dot(left[1, rows], fields[...], preferred_element_type=jnp.float32)

    def term(block, source):
        rows = pl.ds(pl.multiple_of(source * SLOTS, SLOTS), SLOTS)
        block = block.astype(jnp.float32)
        both = product[0, rows] * block[:, :span] - product[1, rows] * block[:, span:]
        return both[:, :cells] + both[:, cells : 2 * cells] + both[:, 2 * cells :]

    total[...] = term(outgoing[me], me)

    @pl.loop(0, SIDE)
    def _(step):
        z = lax.rem(my_z - zigzag(step) + SIDE, SIDE)

        @pl.loop(0, SIDE)
        def _(inner):
            y = lax.rem(my_y - zigzag(inner) + SIDE, SIDE)
            source = z * SIDE + y

            @pl.when(source != me)
            def _():
                block_copy(source, source).wait_recv()
                total[...] += term(incoming[source], source)

    partial[...] = jnp.sum(total[...], axis=0, keepdims=True)

    def sum_copy(other, row):
        return pltpu.make_async_remote_copy(
            src_ref=partial,
            dst_ref=gathered.at[row],
            send_sem=sum_send_sem.at[other],
            recv_sem=sum_recv_sem.at[row],
            device_id={"freq": other},
            device_id_type=MESH,
        )

    @pl.loop(1, freqs)
    def _(k):
        sum_copy(lax.rem(mine + k, freqs), mine).start()

    gathered[mine] = partial[...]

    @pl.loop(1, bricks)
    def _(k):
        other = lax.rem(me + k, bricks)
        label_copy(other, me).wait_send()
        block_copy(other, me).wait_send()

    @pl.loop(1, freqs)
    def _(k):
        other = lax.rem(mine + k, freqs)
        sum_copy(other, other).wait_recv()
        sum_copy(other, mine).wait_send()

    result = gathered[0]
    for row in range(1, freqs):
        result = result + gathered[row]
    out_ref[...] = result


def on_device(
    forward_fields, adjoint_panels, residual_blocks, residual_columns, panel_brick, panel_receiver
):
    bricks, freqs = lax.axis_size("brick"), lax.axis_size("freq")
    held, span = adjoint_panels.shape[1], adjoint_panels.shape[3]
    cells = span // 3
    tx = forward_fields.shape[3]
    panels = adjoint_panels[0].reshape(held, 2 * span)
    fields = forward_fields[0, 0].reshape(2 * tx, span)
    blocks = residual_blocks[0, 0]
    slots = bricks * SLOTS
    any_space = pl.BlockSpec(memory_space=pl.ANY)
    vmem = pl.BlockSpec(memory_space=pltpu.VMEM)
    summed = pl.pallas_call(
        functools.partial(kernel, bricks, freqs),
        out_shape=jax.ShapeDtypeStruct((1, cells), jnp.float32),
        in_specs=[
            pl.BlockSpec(memory_space=pltpu.SMEM), vmem, vmem, any_space, any_space, any_space,
        ],
        out_specs=vmem,
        scratch_shapes=[
            pltpu.VMEM(panels.shape, jnp.bfloat16),
            pltpu.VMEM(fields.shape, jnp.bfloat16),
            pltpu.VMEM(blocks.shape, jnp.bfloat16),
            pltpu.VMEM((bricks, SLOTS, 2 * span), jnp.bfloat16),
            pltpu.VMEM((bricks, SLOTS, 2 * span), jnp.bfloat16),
            pltpu.VMEM((bricks, 128), jnp.int32),
            pltpu.VMEM((bricks, 128), jnp.int32),
            pltpu.VMEM((2, tx, 512), jnp.bfloat16),
            pltpu.VMEM((2, slots, 2 * tx), jnp.bfloat16),
            pltpu.VMEM((2, slots, span), jnp.float32),
            pltpu.VMEM((SLOTS, cells), jnp.float32),
            pltpu.VMEM((1, cells), jnp.float32),
            pltpu.VMEM((freqs, 1, cells), jnp.float32),
            pltpu.SemaphoreType.DMA((3,)),
            pltpu.SemaphoreType.DMA((bricks,)),
            pltpu.SemaphoreType.DMA((bricks,)),
            pltpu.SemaphoreType.DMA((bricks,)),
            pltpu.SemaphoreType.DMA((bricks,)),
            pltpu.SemaphoreType.DMA((freqs,)),
            pltpu.SemaphoreType.DMA((freqs,)),
        ],
        compiler_params=pltpu.CompilerParams(collective_id=0, has_side_effects=True),
        name="exchange_and_correlate",
    )(
        residual_columns[0],
        panel_brick.reshape(1, held),
        panel_receiver.reshape(1, held),
        panels,
        fields,
        blocks,
    )
    share = cells // freqs
    return lax.dynamic_slice_in_dim(summed[0], lax.axis_index("freq") * share, share, 0)


def solution(mesh):
    placed = (
        P("freq", "brick", None, None, None),
        P("freq", "brick", None, None),
        P("freq", "brick", None, None, None, None),
        P("brick", None, None),
        P("brick", None),
        P("brick"),
    )
    return jax.shard_map(
        on_device, mesh=mesh, in_specs=placed, out_specs=P(("brick", "freq")), check_vma=False
    )
```

time: 157 us -> 163 us (1.038)
  the two profiles are of different devices: /device:TPU:112 before, /device:TPU:257 now
where the time goes in v1:
time: 163 us; the launch traced here: 162 us
  Pallas kernels  157 us (96%)
  local copies, waits for them, and re-layouts  5.38 us (3%)
    pallas_call x1, Pallas kernels, on_device(): pl.pallas_call(functools.partial(kernel, bricks, freqs), out_shape=jax.Sh...  157 us

profile of v1, /device:TPU:257, one launch (start us, length us, event | category | flops | bytes accessed | tf_op | source)
XLA Modules:
  0.0 162.5 jit_solution(14209463092147972816)
XLA Ops:
  0.0 1.3 copy.8
  1.3 2.8 %copy.9 = bf16[32,8,2,1536]{3,1,2,0:T(8,128)(2,1)} copy(bf16[32,8,2,1536]{3,2,1,0:T(2,128)(2,1)} %bitcast.12) | data formatting | bytes 3145728
  4.1 157.1 %exchange_and_correlate.1 = f32[1,512]{1,0:T(1,128)} custom-call(s32[8,3]{1,0:T(8,128)} %bitcast.14, s32[1,256]{1,0:T(1,128)} %bitcast.15, s32[1,256]{1,0:T(1,128)} %bitcast.16, bf16[256,3072]{1,0:T(8,128)(2,1)} %bitcast.10, bf16[1024,1536]{1,0:T(8,128)(2,1)} %bitcast.11, bf16[8,3,64,128]{3,2,1,0:T(8,128)(2,1)} %bitcast.13), custom_call_target="tpu_custom_call" | custom-call | tf_op jit(solution)/shard_map/exchange_and_correlate/pallas_call | solution.py:240
  161.2 1.3 dynamic-slice_bitcast_fusion

commit v2 on v1

v2 whole, which is shorter than its diff:
```python
import functools

import jax
import jax.numpy as jnp
from jax import lax
from jax.experimental import pallas as pl
from jax.experimental.pallas import tpu as pltpu
from jax.sharding import PartitionSpec as P

SIDE = 8
SLOTS = 8
MESH = pl.DeviceIdType.MESH


def zigzag(step):
    half = (step + 1) // 2
    return 4 + half * (1 - 2 * lax.rem(step, 2))


def kernel(
    freqs, columns_ref, target_ref, receiver_ref, panels_hbm, fields_hbm, blocks_hbm,
    out_ref,
    panels, fields, blocks, out_a, out_b, mid_a, mid_b, in_a, in_b, labels_own, labels_mid,
    labels_in, dense, left, product, total, partial, gathered,
    load_sem, label_send1, label_recv1, label_send2, label_recv2,
    send1_a, recv1_a, send1_b, recv1_b, send2_a, recv2_a, send2_b, recv2_b,
    sum_send_sem, sum_recv_sem,
):
    me = lax.axis_index("brick")
    mine = lax.axis_index("freq")
    z, y = me // SIDE, lax.rem(me, SIDE)
    held = panels.shape[0]
    span = fields.shape[1]
    cells = span // 3
    tx = fields.shape[0] // 2

    def remote(src, dst, send, recv, **where):
        return pltpu.make_async_remote_copy(
            src_ref=src, dst_ref=dst, send_sem=send, recv_sem=recv,
            device_id=where, device_id_type=MESH,
        )

    def at(row, column):
        return row * SIDE + column

    def around(here, step):
        return lax.rem(here + zigzag(step), SIDE)

    def back(here, step):
        return lax.rem(here - zigzag(step) + SIDE, SIDE)

    loads = [
        pltpu.make_async_copy(panels_hbm, panels, load_sem.at[0]),
        pltpu.make_async_copy(blocks_hbm, blocks, load_sem.at[1]),
        pltpu.make_async_copy(fields_hbm, fields, load_sem.at[2]),
    ]
    for load in loads:
        load.start()

    barrier = pltpu.get_barrier_semaphore()

    @pl.loop(1, SIDE)
    def _(k):
        other_z, other_y = lax.rem(z + k, SIDE), lax.rem(y + k, SIDE)
        pl.semaphore_signal(
            barrier, inc=1, device_id={"brick": at(other_z, y)}, device_id_type=MESH
        )
        pl.semaphore_signal(
            barrier, inc=1, device_id={"brick": at(z, other_y)}, device_id_type=MESH
        )

    @pl.loop(1, freqs)
    def _(k):
        pl.semaphore_signal(
            barrier, inc=1, device_id={"freq": lax.rem(mine + k, freqs)}, device_id_type=MESH
        )

    target = target_ref[...]
    down = lax.broadcasted_iota(jnp.int32, (held, held), 0)
    across = lax.broadcasted_iota(jnp.int32, (held, held), 1)
    diagonal = down == across
    target_col = jnp.sum(jnp.where(diagonal, target, 0), axis=1, keepdims=True)
    same = target_col == target
    rank = jnp.sum(jnp.where(same & (down < across), 1, 0), axis=0, keepdims=True)
    rank_col = jnp.sum(jnp.where(same & (across < down), 1, 0), axis=1, keepdims=True)
    target_z, target_y = target // SIDE, lax.rem(target, SIDE)
    place_a = target * SLOTS + rank
    place_b = (target_y * SIDE + target_z) * SLOTS + rank

    value = receiver_ref[...] + 1
    names = lax.broadcasted_iota(jnp.int32, (SIDE, held), 0) == target_z
    lanes = lax.broadcasted_iota(jnp.int32, (held, 128), 1)
    by_lane = lax.rem(target_col, SIDE) * SLOTS + rank_col == lanes
    by_lane = by_lane.astype(jnp.float32).astype(jnp.bfloat16)
    high = jnp.where(names, value // 16, 0).astype(jnp.float32).astype(jnp.bfloat16)
    low = jnp.where(names, lax.rem(value, 16), 0).astype(jnp.float32).astype(jnp.bfloat16)
    high = jnp.dot(high, by_lane, preferred_element_type=jnp.float32)
    low = jnp.dot(low, by_lane, preferred_element_type=jnp.float32)
    labels_own[...] = (high * 16.0 + low).astype(jnp.int32)

    def label_copy1(other, row):
        return remote(
            labels_own.at[pl.ds(other, 1)], labels_mid.at[pl.ds(row, 1)],
            label_send1.at[other], label_recv1.at[row], brick=at(other, y),
        )

    def label_copy2(other, row):
        return remote(
            labels_mid, labels_in.at[row],
            label_send2.at[other], label_recv2.at[row], brick=at(z, other),
        )

    def first_a(other, row):
        return remote(
            out_a.at[other], mid_a.at[row], send1_a.at[other], recv1_a.at[row],
            brick=at(other, y),
        )

    def first_b(other, row):
        return remote(
            out_b.at[other], mid_b.at[row], send1_b.at[other], recv1_b.at[row],
            brick=at(z, other),
        )

    def second_a(block, source, other, column):
        index = at(column, source)
        return remote(
            block.at[other], in_a.at[index], send2_a.at[at(source, other)], recv2_a.at[index],
            brick=at(z, other),
        )

    def second_b(block, source, other, row):
        index = at(source, row)
        return remote(
            block.at[other], in_b.at[index], send2_b.at[at(source, other)], recv2_b.at[index],
            brick=at(other, y),
        )

    def build(group, place, part, into):
        slots = lax.broadcasted_iota(jnp.int32, (SIDE * SLOTS, held), 0) + group * (SIDE * SLOTS)
        select = (slots == place).astype(jnp.float32).astype(jnp.bfloat16)
        rows = jnp.dot(
            select, panels[:, part * span : (part + 1) * span],
            preferred_element_type=jnp.float32,
        )
        into[group] = rows.reshape(SIDE, SLOTS, span).astype(jnp.bfloat16)

    loads[0].wait()
    build(around(z, 0), place_a, 0, out_a)
    build(around(y, 0), place_b, 1, out_b)
    pl.semaphore_wait(barrier, 2 * (SIDE - 1) + freqs - 1)

    @pl.loop(1, SIDE)
    def _(k):
        label_copy1(lax.rem(z + k, SIDE), z).start()

    @pl.loop(0, SIDE)
    def _(step):
        other_z, other_y = around(z, step), around(y, step)

        @pl.when(step > 0)
        def _():
            build(other_z, place_a, 0, out_a)
            build(other_y, place_b, 1, out_b)

        @pl.when(step < SIDE - 1)
        def _():
            first_a(other_z, z).start()
            first_b(other_y, y).start()

    @pl.loop(0, SIDE - 1)
    def _(step):
        second_a(out_a.at[z], z, around(y, step), y).start()
        second_b(out_b.at[y], y, around(z, step), z).start()

    labels_mid[pl.ds(z, 1)] = labels_own[pl.ds(z, 1)]

    @pl.loop(1, SIDE)
    def _(k):
        other = lax.rem(z + k, SIDE)
        label_copy1(other, other).wait_recv()

    @pl.loop(1, SIDE)
    def _(k):
        label_copy2(lax.rem(y + k, SIDE), y).start()

    labels_in[y] = labels_mid[...]

    loads[1].wait()
    for k in range(columns_ref.shape[0]):
        for r in range(SIDE):
            tile = jnp.zeros((blocks.shape[2], blocks.shape[3]), jnp.bfloat16)
            for j in range(columns_ref.shape[1]):
                tile = jnp.where(columns_ref[k, j] == r, blocks[k, j], tile)
            dense[0, pl.ds(k * 64, 64), pl.ds(r * 64, 64)] = tile[:, :64]
            dense[1, pl.ds(k * 64, 64), pl.ds(r * 64, 64)] = tile[:, 64:]

    @pl.loop(1, SIDE)
    def _(k):
        other = lax.rem(y + k, SIDE)
        label_copy2(other, other).wait_recv()

    slots = SIDE * SIDE * SLOTS
    named = labels_in[...].reshape(SIDE * SIDE, 128)
    pick = lax.broadcasted_iota(jnp.int32, (SIDE * SIDE, SLOTS, 128), 1) + y * SLOTS
    pick = pick == lax.broadcasted_iota(jnp.int32, (SIDE * SIDE, SLOTS, 128), 2)
    label = jnp.sum(jnp.where(pick, named[:, None, :], 0), axis=2, keepdims=True)
    label = label.reshape(slots, 1) - 1
    receivers = lax.broadcasted_iota(jnp.int32, (slots, dense.shape[2]), 1)
    onehot = (receivers == label).astype(jnp.float32).astype(jnp.bfloat16)
    dims = (((1,), (1,)), ((), ()))
    real = lax.dot_general(onehot, dense[0], dims, preferred_element_type=jnp.float32)
    imag = lax.dot_general(onehot, dense[1], dims, preferred_element_type=jnp.float32)
    left[0, :, pl.ds(0, tx)] = real.astype(jnp.bfloat16)
    left[0, :, pl.ds(tx, tx)] = (-imag).astype(jnp.bfloat16)
    left[1, :, pl.ds(0, tx)] = imag.astype(jnp.bfloat16)
    left[1, :, pl.ds(tx, tx)] = real.astype(jnp.bfloat16)

    loads[2].wait()

    @pl.loop(0, 4)
    def _(tile):
        rows = pl.ds(pl.multiple_of(tile * 128, 128), 128)
        product[0, rows] = jnp.dot(left[0, rows], fields[...], preferred_element_type=jnp.float32)
        product[1, rows] = jnp.dot(left[1, rows], fields[...], preferred_element_type=jnp.float32)

    def term(part, block, index):
        rows = pl.ds(pl.multiple_of(index * SLOTS, SLOTS), SLOTS)
        both = product[part, rows] * block.astype(jnp.float32)
        return both[:, :cells] + both[:, cells : 2 * cells] + both[:, 2 * cells :]

    total[...] = term(0, out_a[z, y], at(y, z)) - term(1, out_b[y, z], at(y, z))

    @pl.loop(0, SIDE - 1)
    def _(step):
        source_z, source_y = back(z, step), back(y, step)
        first_a(source_z, source_z).wait_recv()

        @pl.loop(0, SIDE - 1)
        def _(inner):
            second_a(mid_a.at[source_z], source_z, around(y, inner), y).start()

        first_b(source_y, source_y).wait_recv()

        @pl.loop(0, SIDE - 1)
        def _(inner):
            second_b(mid_b.at[source_y], source_y, around(z, inner), z).start()

        total[...] += term(0, mid_a[source_z, y], at(y, source_z)) - term(
            1, mid_b[source_y, z], at(source_y, z)
        )

    @pl.loop(0, SIDE)
    def _(step):
        source = lax.rem(step + SIDE - 1, SIDE)
        source_z, source_y = back(z, source), back(y, source)

        @pl.loop(0, SIDE - 1)
        def _(inner):
            column, row = back(y, inner), back(z, inner)
            index_a, index_b = at(column, source_z), at(source_y, row)
            second_a(mid_a.at[source_z], source_z, column, column).wait_recv()
            second_b(mid_b.at[source_y], source_y, row, row).wait_recv()
            total[...] += term(0, in_a[index_a], index_a) - term(1, in_b[index_b], index_b)

    partial[...] = jnp.sum(total[...], axis=0, keepdims=True)

    def sum_copy(other, row):
        return remote(
            partial, gathered.at[row], sum_send_sem.at[other], sum_recv_sem.at[row], freq=other
        )

    @pl.loop(1, freqs)
    def _(k):
        sum_copy(lax.rem(mine + k, freqs), mine).start()

    gathered[mine] = partial[...]

    @pl.loop(1, SIDE)
    def _(k):
        other_z, other_y = lax.rem(z + k, SIDE), lax.rem(y + k, SIDE)
        label_copy1(other_z, z).wait_send()
        label_copy2(other_y, y).wait_send()
        first_a(other_z, z).wait_send()
        first_b(other_y, y).wait_send()

        @pl.loop(0, SIDE)
        def _(source):
            second_a(mid_a.at[source], source, other_y, y).wait_send()
            second_b(mid_b.at[source], source, other_z, z).wait_send()

    @pl.loop(1, freqs)
    def _(k):
        other = lax.rem(mine + k, freqs)
        sum_copy(other, other).wait_recv()
        sum_copy(other, mine).wait_send()

    result = gathered[0]
    for row in range(1, freqs):
        result = result + gathered[row]
    out_ref[...] = result


def on_device(
    forward_fields, adjoint_panels, residual_blocks, residual_columns, panel_brick, panel_receiver
):
    bricks, freqs = lax.axis_size("brick"), lax.axis_size("freq")
    held, span = adjoint_panels.shape[1], adjoint_panels.shape[3]
    cells = span // 3
    tx = forward_fields.shape[3]
    panels = adjoint_panels[0].reshape(held, 2 * span)
    fields = forward_fields[0, 0].reshape(2 * tx, span)
    blocks = residual_blocks[0, 0]
    slots = bricks * SLOTS
    half = (SIDE, SIDE, SLOTS, span)
    any_space = pl.BlockSpec(memory_space=pl.ANY)
    vmem = pl.BlockSpec(memory_space=pltpu.VMEM)
    summed = pl.pallas_call(
        functools.partial(kernel, freqs),
        out_shape=jax.ShapeDtypeStruct((1, cells), jnp.float32),
        in_specs=[
            pl.BlockSpec(memory_space=pltpu.SMEM), vmem, vmem, any_space, any_space, any_space,
        ],
        out_specs=vmem,
        scratch_shapes=[
            pltpu.VMEM(panels.shape, jnp.bfloat16),
            pltpu.VMEM(fields.shape, jnp.bfloat16),
            pltpu.VMEM(blocks.shape, jnp.bfloat16),
            pltpu.VMEM(half, jnp.bfloat16),
            pltpu.VMEM(half, jnp.bfloat16),
            pltpu.VMEM(half, jnp.bfloat16),
            pltpu.VMEM(half, jnp.bfloat16),
            pltpu.VMEM((bricks, SLOTS, span), jnp.bfloat16),
            pltpu.VMEM((bricks, SLOTS, span), jnp.bfloat16),
            pltpu.VMEM((SIDE, 128), jnp.int32),
            pltpu.VMEM((SIDE, 128), jnp.int32),
            pltpu.VMEM((SIDE, SIDE, 128), jnp.int32),
            pltpu.VMEM((2, tx, 512), jnp.bfloat16),
            pltpu.VMEM((2, slots, 2 * tx), jnp.bfloat16),
            pltpu.VMEM((2, slots, span), jnp.float32),
            pltpu.VMEM((SLOTS, cells), jnp.float32),
            pltpu.VMEM((1, cells), jnp.float32),
            pltpu.VMEM((freqs, 1, cells), jnp.float32),
            pltpu.SemaphoreType.DMA((3,)),
            *[pltpu.SemaphoreType.DMA((SIDE,))] * 8,
            *[pltpu.SemaphoreType.DMA((bricks,))] * 4,
            pltpu.SemaphoreType.DMA((freqs,)),
            pltpu.SemaphoreType.DMA((freqs,)),
        ],
        compiler_params=pltpu.CompilerParams(collective_id=0, has_side_effects=True),
        name="exchange_and_correlate",
    )(
        residual_columns[0],
        panel_brick.reshape(1, held),
        panel_receiver.reshape(1, held),
        panels,
        fields,
        blocks,
    )
    share = cells // freqs
    return lax.dynamic_slice_in_dim(summed[0], lax.axis_index("freq") * share, share, 0)


def solution(mesh):
    placed = (
        P("freq", "brick", None, None, None),
        P("freq", "brick", None, None),
        P("freq", "brick", None, None, None, None),
        P("brick", None, None),
        P("brick", None),
        P("brick"),
    )
    return jax.shard_map(
        on_device, mesh=mesh, in_specs=placed, out_specs=P(("brick", "freq")), check_vma=False
    )
```

time: 163 us -> 107 us (0.66)
  the two profiles are of different devices: /device:TPU:257 before, /device:TPU:1 now
where the time goes in v2:
time: 107 us
  Pallas kernels  102 us (95%)
  local copies, waits for them, and re-layouts  5.38 us (5%)
    pallas_call x1, Pallas kernels, on_device(): pl.pallas_call(functools.partial(kernel, freqs), out_shape=jax.ShapeDtype...  102 us
    unnamed x1, local copies, waits for them, and re-layouts  2.78 us

profile of v2, /device:TPU:1, one launch (start us, length us, event | category | flops | bytes accessed | tf_op | source)
XLA Modules:
  0.0 107.0 jit_solution(6727869979477914235)
XLA Ops:
  0.0 1.3 %copy.8 = s32[1,8,3]{2,1,0:T(8,128)} copy(s32[1,8,3]{1,0,2:T(1,128)} %param.9) | data formatting | bytes 192 | tf_op jit(solution)/shard_map/squeeze | solution.py:353
  1.3 2.8 %copy.9 = bf16[32,8,2,1536]{3,1,2,0:T(8,128)(2,1)} copy(bf16[32,8,2,1536]{3,2,1,0:T(2,128)(2,1)} %bitcast.12) | data formatting | bytes 3145728
  4.1 101.6 %exchange_and_correlate.1 = f32[1,512]{1,0:T(1,128)} custom-call(s32[8,3]{1,0:T(8,128)} %bitcast.14, s32[1,256]{1,0:T(1,128)} %bitcast.15, s32[1,256]{1,0:T(1,128)} %bitcast.16, bf16[256,3072]{1,0:T(8,128)(2,1)} %bitcast.10, bf16[1024,1536]{1,0:T(8,128)(2,1)} %bitcast.11, bf16[8,3,64,128]{3,2,1,0:T(8,128)(2,1)} %bitcast.13), custom_call_target="tpu_custom_call" | custom-call | tf_op jit(solution)/shard_map/exchange_and_correlate/pallas_call | solution.py:318
  105.7 1.3 %dynamic-slice_bitcast_fusion = f32[64]{0:T(128)} fusion(f32[1,512]{1,0:T(1,128)} %exchange_and_correlate.1, s32[]{:T(128)S(6)} %select_n.3), kind=kLoop, calls=%fused_computation | loop fusion | bytes 516 | tf_op jit(solution)/shard_map/dynamic_slice | solution.py:361

commit v3 on v2

--- a/solution.py
+++ b/solution.py
@@ -20,7 +20,7 @@
 def kernel(
     freqs, columns_ref, target_ref, receiver_ref, panels_hbm, fields_hbm, blocks_hbm,
     out_ref,
-    panels, fields, blocks, out_a, out_b, mid_a, mid_b, in_a, in_b, labels_own, labels_mid,
+    stored, panels, fields, blocks, out_a, out_b, mid_a, mid_b, in_a, in_b, labels_own, labels_mid,
     labels_in, dense, left, product, total, partial, gathered,
     load_sem, label_send1, label_recv1, label_send2, label_recv2,
     send1_a, recv1_a, send1_b, recv1_b, send2_a, recv2_a, send2_b, recv2_b,
@@ -29,7 +29,7 @@
     me = lax.axis_index("brick")
     mine = lax.axis_index("freq")
     z, y = me // SIDE, lax.rem(me, SIDE)
-    held = panels.shape[0]
+    held = panels.shape[1]
     span = fields.shape[1]
     cells = span // 3
     tx = fields.shape[0] // 2
@@ -50,7 +50,7 @@
         return lax.rem(here - zigzag(step) + SIDE, SIDE)
 
     loads = [
-        pltpu.make_async_copy(panels_hbm, panels, load_sem.at[0]),
+        pltpu.make_async_copy(panels_hbm, stored, load_sem.at[0]),
         pltpu.make_async_copy(blocks_hbm, blocks, load_sem.at[1]),
         pltpu.make_async_copy(fields_hbm, fields, load_sem.at[2]),
     ]
@@ -140,12 +140,12 @@
         slots = lax.broadcasted_iota(jnp.int32, (SIDE * SLOTS, held), 0) + group * (SIDE * SLOTS)
         select = (slots == place).astype(jnp.float32).astype(jnp.bfloat16)
         rows = jnp.dot(
-            select, panels[:, part * span : (part + 1) * span],
-            preferred_element_type=jnp.float32,
+            select, panels[part], preferred_element_type=jnp.float32,
         )
         into[group] = rows.reshape(SIDE, SLOTS, span).astype(jnp.bfloat16)
 
     loads[0].wait()
+    panels[...] = jnp.swapaxes(stored[...], 0, 1)
     build(around(z, 0), place_a, 0, out_a)
     build(around(y, 0), place_b, 1, out_b)
     pl.semaphore_wait(barrier, 2 * (SIDE - 1) + freqs - 1)
@@ -187,11 +187,11 @@
     labels_in[y] = labels_mid[...]
 
     loads[1].wait()
-    for k in range(columns_ref.shape[0]):
+    for k in range(columns_ref.shape[2]):
         for r in range(SIDE):
             tile = jnp.zeros((blocks.shape[2], blocks.shape[3]), jnp.bfloat16)
-            for j in range(columns_ref.shape[1]):
-                tile = jnp.where(columns_ref[k, j] == r, blocks[k, j], tile)
+            for j in range(columns_ref.shape[0]):
+                tile = jnp.where(columns_ref[j, 0, k] == r, blocks[k, j], tile)
             dense[0, pl.ds(k * 64, 64), pl.ds(r * 64, 64)] = tile[:, :64]
             dense[1, pl.ds(k * 64, 64), pl.ds(r * 64, 64)] = tile[:, 64:]
 
@@ -218,19 +218,18 @@
 
     loads[2].wait()
 
-    @pl.loop(0, 4)
-    def _(tile):
+    def multiply(piece):
+        part, tile = piece // 4, lax.rem(piece, 4)
         rows = pl.ds(pl.multiple_of(tile * 128, 128), 128)
-        product[0, rows] = jnp.dot(left[0, rows], fields[...], preferred_element_type=jnp.float32)
-        product[1, rows] = jnp.dot(left[1, rows], fields[...], preferred_element_type=jnp.float32)
+        product[part, rows] = jnp.dot(
+            left[part, rows], fields[...], preferred_element_type=jnp.float32
+        )
 
     def term(part, block, index):
         rows = pl.ds(pl.multiple_of(index * SLOTS, SLOTS), SLOTS)
         both = product[part, rows] * block.astype(jnp.float32)
         return both[:, :cells] + both[:, cells : 2 * cells] + both[:, 2 * cells :]
 
-    total[...] = term(0, out_a[z, y], at(y, z)) - term(1, out_b[y, z], at(y, z))
-
     @pl.loop(0, SIDE - 1)
     def _(step):
         source_z, source_y = back(z, step), back(y, step)
@@ -246,6 +245,14 @@
         def _(inner):
             second_b(mid_b.at[source_y], source_y, around(z, inner), z).start()
 
+        multiply(step)
+
+    multiply(SIDE - 1)
+    total[...] = term(0, out_a[z, y], at(y, z)) - term(1, out_b[y, z], at(y, z))
+
+    @pl.loop(0, SIDE - 1)
+    def _(step):
+        source_z, source_y = back(z, step), back(y, step)
         total[...] += term(0, mid_a[source_z, y], at(y, source_z)) - term(
             1, mid_b[source_y, z], at(source_y, z)
         )
@@ -308,7 +315,6 @@
     held, span = adjoint_panels.shape[1], adjoint_panels.shape[3]
     cells = span // 3
     tx = forward_fields.shape[3]
-    panels = adjoint_panels[0].reshape(held, 2 * span)
     fields = forward_fields[0, 0].reshape(2 * tx, span)
     blocks = residual_blocks[0, 0]
     slots = bricks * SLOTS
@@ -323,7 +329,8 @@
         ],
         out_specs=vmem,
         scratch_shapes=[
-            pltpu.VMEM(panels.shape, jnp.bfloat16),
+            pltpu.VMEM((held, 2, span), jnp.bfloat16),
+            pltpu.VMEM((2, held, span), jnp.bfloat16),
             pltpu.VMEM(fields.shape, jnp.bfloat16),
             pltpu.VMEM(blocks.shape, jnp.bfloat16),
             pltpu.VMEM(half, jnp.bfloat16),
@@ -350,10 +357,10 @@
         compiler_params=pltpu.CompilerParams(collective_id=0, has_side_effects=True),
         name="exchange_and_correlate",
     )(
-        residual_columns[0],
+        residual_columns.transpose(2, 0, 1),
         panel_brick.reshape(1, held),
         panel_receiver.reshape(1, held),
-        panels,
+        adjoint_panels[0],
         fields,
         blocks,
     )

time: 107 us -> 98.9 us (0.924)
  Pallas kernels: 102 us -> 97.5 us
  local copies, waits for them, and re-layouts: 5.38 us -> 1.27 us
    pallas_call x1, Pallas kernels: 102 us -> 97.5 us  [on_device(): pl.pallas_call(functools.partial(kernel, freqs), out_shape=jax.ShapeDtype...]
    unnamed x1 -> x0, local copies, waits for them, and re-layouts: 2.78 us -> none
    squeeze x1 -> x0, local copies, waits for them, and re-layouts: 1.34 us -> none  [on_device(): residual_columns[0]]
where the time goes in v3:
time: 98.9 us; the launch traced here: 98.8 us
  Pallas kernels  97.5 us (99%)
  local copies, waits for them, and re-layouts  1.27 us (1%)
    pallas_call x1, Pallas kernels, on_device(): pl.pallas_call(functools.partial(kernel, freqs), out_shape=jax.ShapeDtype...  97.5 us

profile of v3, /device:TPU:1, one launch (start us, length us, event | category | flops | bytes accessed | tf_op | source)
XLA Modules:
  0.0 98.8 jit_solution(13730209931632145593)
XLA Ops:
  0.0 97.5 %exchange_and_correlate.1 = f32[1,512]{1,0:T(1,128)} custom-call(s32[3,1,8]{2,1,0:T(1,128)} %bitcast.11, s32[1,256]{1,0:T(1,128)} %bitcast.12, s32[1,256]{1,0:T(1,128)} %bitcast.13, bf16[256,2,1536]{2,1,0:T(2,128)(2,1)} %bitcast.9, bf16[1024,1536]{1,0:T(8,128)(2,1)} %bitcast.8, bf16[8,3,64,128]{3,2,1,0:T(8,128)(2,1)} %bitcast.10), custom_call_target="tpu_custom_call" | custom-call | tf_op jit(solution)/shard_map/exchange_and_correlate/pallas_call | solution.py:324
  97.5 1.3 %dynamic-slice_bitcast_fusion = f32[64]{0:T(128)} fusion(f32[1,512]{1,0:T(1,128)} %exchange_and_correlate.1, s32[]{:T(128)S(6)} %select_n.3), kind=kLoop, calls=%fused_computation | loop fusion | bytes 516 | tf_op jit(solution)/shard_map/dynamic_slice | solution.py:368

commit v4 on v3

--- a/solution.py
+++ b/solution.py
@@ -10,6 +10,10 @@
 SIDE = 8
 SLOTS = 8
 MESH = pl.DeviceIdType.MESH
+CAPS = (128, 112, 80, 48)
+EDGES = (0, 48, 80, 112, 128)
+STEPS = len(CAPS)
+START_LANE, SPLIT_LANE, FLAG_LANE = 64, 65, 127
 
 
 def zigzag(step):
@@ -17,7 +21,7 @@
     return 4 + half * (1 - 2 * lax.rem(step, 2))
 
 
-def kernel(
+def padded_kernel(
     freqs, columns_ref, target_ref, receiver_ref, panels_hbm, fields_hbm, blocks_hbm,
     out_ref,
     stored, panels, fields, blocks, out_a, out_b, mid_a, mid_b, in_a, in_b, labels_own, labels_mid,
@@ -308,6 +312,396 @@
     out_ref[...] = result
 
 
+def count(mask, axis):
+    return jnp.sum(jnp.where(mask, 1, 0), axis=axis, keepdims=True)
+
+
+def iota(shape, axis):
+    return lax.broadcasted_iota(jnp.int32, shape, axis)
+
+
+def onehot(mask):
+    return mask.astype(jnp.float32).astype(jnp.bfloat16)
+
+
+def make_lists(axis_row, axis_col, slot_row, slot_col, here):
+    off_row = lax.rem(axis_row - here + SIDE, SIDE)
+    off_col = lax.rem(axis_col - here + SIDE, SIDE)
+    half = SIDE // 2
+    far_row, far_col = off_row == half, off_col == half
+    index_row = count(far_col & (slot_col < slot_row), 0)
+    index_col = count(far_row & (slot_row < slot_col), 1)
+    number = count(far_row, 1)
+    up = count((off_row >= 1) & (off_row < half), 1)
+    down = count(off_row > half, 1)
+    split = jnp.minimum(jnp.maximum(down + number - up, 0) // 2, number)
+
+    def which(off, index):
+        plus = ((off >= 1) & (off < half)) | ((off == half) & (index < split))
+        minus = (off > half) | ((off == half) & (index >= split))
+        return jnp.where(plus, 0, jnp.where(minus, 1, 2))
+
+    list_row, list_col = which(off_row, index_row), which(off_col, index_col)
+    dist_row = jnp.minimum(off_row, SIDE - off_row)
+    dist_col = jnp.minimum(off_col, SIDE - off_col)
+    key_row = (half - dist_row) * (SIDE * SLOTS) + slot_row
+    key_col = (half - dist_col) * (SIDE * SLOTS) + slot_col
+    place = count((list_col == list_row) & (key_col < key_row), 0)
+
+    over = jnp.zeros((1, 1), jnp.int32)
+    for one in range(2):
+        for step in range(STEPS):
+            length = count((list_row == one) & (dist_row > step), 1)
+            over = jnp.maximum(over, jnp.where(length > CAPS[step], 1, 0))
+
+    row = lax.rem(iota((SIDE, 1), 0) - here + SIDE, SIDE)
+    row_list = jnp.where(row < half, 0, 1)
+    row_dist = jnp.minimum(row, SIDE - row)
+    start = count((list_row == row_list) & (dist_row > row_dist), 1)
+    return list_row, place, start, split, over
+
+
+def compact_kernel(
+    freqs, columns_ref, target_ref, receiver_ref, panels_hbm, fields_hbm, blocks_hbm,
+    out_ref, flag_ref,
+    stored, panels, fields, blocks, lists, ring1, ring2, ring3, ring4, mid_a, mid_b, in_a, in_b,
+    labels_own, labels_mid, labels_in, dense, left, product, total, partial, gathered,
+    load_sem, label_send1, label_recv1, label_send2, label_recv2, hop_send, hop_recv,
+    send2_a, recv2_a, send2_b, recv2_b, sum_send_sem, sum_recv_sem,
+):
+    me = lax.axis_index("brick")
+    mine = lax.axis_index("freq")
+    z, y = me // SIDE, lax.rem(me, SIDE)
+    here = (z, y)
+    rings = (ring1, ring2, ring3, ring4)
+    mids = (mid_a, mid_b)
+    held = panels.shape[1]
+    span = fields.shape[1]
+    cells = span // 3
+    tx = fields.shape[0] // 2
+    group = SIDE * SLOTS
+
+    def remote(src, dst, send, recv, **where):
+        return pltpu.make_async_remote_copy(
+            src_ref=src, dst_ref=dst, send_sem=send, recv_sem=recv,
+            device_id=where, device_id_type=MESH,
+        )
+
+    def at(row, column):
+        return row * SIDE + column
+
+    def along(path, other):
+        return at(other, y) if path == 0 else at(z, other)
+
+    def around(start, step):
+        return lax.rem(start + zigzag(step), SIDE)
+
+    def back(start, step):
+        return lax.rem(start - zigzag(step) + SIDE, SIDE)
+
+    loads = [
+        pltpu.make_async_copy(panels_hbm, stored, load_sem.at[0]),
+        pltpu.make_async_copy(blocks_hbm, blocks, load_sem.at[1]),
+        pltpu.make_async_copy(fields_hbm, fields, load_sem.at[2]),
+    ]
+    for load in loads:
+        load.start()
+
+    barrier = pltpu.get_barrier_semaphore()
+
+    @pl.loop(1, SIDE)
+    def _(k):
+        for path in range(2):
+            other = lax.rem(here[path] + k, SIDE)
+            pl.semaphore_signal(
+                barrier, inc=1, device_id={"brick": along(path, other)}, device_id_type=MESH
+            )
+
+    @pl.loop(1, freqs)
+    def _(k):
+        pl.semaphore_signal(
+            barrier, inc=1, device_id={"freq": lax.rem(mine + k, freqs)}, device_id_type=MESH
+        )
+
+    target = target_ref[...]
+    down, across = iota((held, held), 0), iota((held, held), 1)
+    target_col = jnp.sum(jnp.where(down == across, target, 0), axis=1, keepdims=True)
+    same = target_col == target
+    rank, rank_col = count(same & (down < across), 0), count(same & (across < down), 1)
+    axis_row = (target // SIDE, lax.rem(target, SIDE))
+    axis_col = (target_col // SIDE, lax.rem(target_col, SIDE))
+    slot_row = tuple(axis_row[1 - path] * SLOTS + rank for path in range(2))
+    slot_col = tuple(axis_col[1 - path] * SLOTS + rank_col for path in range(2))
+
+    loads[0].wait()
+    panels[...] = jnp.swapaxes(stored[...], 0, 1)
+    value = receiver_ref[...] + 1
+    over = jnp.zeros((1, 1), jnp.int32)
+    lanes = iota((SIDE, 128), 1)
+    rows = []
+    for path in range(2):
+        list_row, place, start, split, too_long = make_lists(
+            axis_row[path], axis_col[path], slot_row[path], slot_col[path], here[path]
+        )
+        over = jnp.maximum(over, too_long)
+        for one in range(2):
+            select = onehot((iota((CAPS[0], held), 0) == place) & (list_row == one))
+            lists[2 * path + one] = jnp.dot(
+                select, panels[path], preferred_element_type=jnp.float32
+            ).astype(jnp.bfloat16)
+        names = iota((SIDE, held), 0) == axis_row[path]
+        by_lane = onehot(slot_col[path] == iota((held, 128), 1))
+        high = jnp.where(names, value // 16, 0).astype(jnp.float32).astype(jnp.bfloat16)
+        low = jnp.where(names, lax.rem(value, 16), 0).astype(jnp.float32).astype(jnp.bfloat16)
+        high = jnp.dot(high, by_lane, preferred_element_type=jnp.float32)
+        low = jnp.dot(low, by_lane, preferred_element_type=jnp.float32)
+        named = (high * 16.0 + low).astype(jnp.int32)
+        named = jnp.where(lanes == START_LANE, start, named)
+        rows.append(jnp.where(lanes == SPLIT_LANE, split, named))
+    labels_own[0] = jnp.where(lanes == FLAG_LANE, over, rows[0])
+    labels_own[1] = rows[1]
+
+    def label_copy1(path, other, row):
+        return remote(
+            labels_own.at[path, pl.ds(other, 1)], labels_mid.at[path, pl.ds(row, 1)],
+            label_send1.at[path, other], label_recv1.at[path, row],
+            brick=along(path, other),
+        )
+
+    def label_copy2(other, row):
+        return remote(
+            labels_mid.at[0], labels_in.at[row],
+            label_send2.at[other], label_recv2.at[row], brick=at(z, other),
+        )
+
+    def hop(path, one, step, chunk):
+        part = 2 * path + one
+        piece = pl.ds(EDGES[chunk], EDGES[chunk + 1] - EDGES[chunk])
+        source = lists if step == 0 else rings[step - 1]
+        index = (part * STEPS + step) * STEPS + chunk
+        other = lax.rem(here[path] + (1 if one == 0 else SIDE - 1), SIDE)
+        return remote(
+            source.at[part, piece], rings[step].at[part, piece],
+            hop_send.at[index], hop_recv.at[index], brick=along(path, other),
+        )
+
+    ways = [(path, one) for path in range(2) for one in range(2)]
+
+    def second_a(source, other, column):
+        index = at(column, source)
+        return remote(
+            mid_a.at[source, other], in_a.at[index],
+            send2_a.at[at(source, other)], recv2_a.at[index], brick=at(z, other),
+        )
+
+    def second_b(source, other, row):
+        index = at(source, row)
+        return remote(
+            mid_b.at[source, other], in_b.at[index],
+            send2_b.at[at(source, other)], recv2_b.at[index], brick=at(other, y),
+        )
+
+    def pass_on(path, source):
+        @pl.loop(0, SIDE - 1)
+        def _(inner):
+            if path == 0:
+                second_a(source, around(y, inner), y).start()
+            else:
+                second_b(source, around(z, inner), z).start()
+
+    def spread(path, step, one):
+        source = lax.rem(here[path] + (SIDE - step - 1 if one == 0 else step + 1), SIDE)
+        row = labels_mid[path, pl.ds(source, 1)]
+        lane, slot = iota((group, 128), 1), iota((group, 128), 0)
+        filled = row > 0
+        full = count((lane == slot) & filled, 1) > 0
+        index = count((lane < slot) & filled, 1)
+        single = iota((1, 128), 1)
+        if step < STEPS - 1:
+            index = index + jnp.sum(jnp.where(single == START_LANE, row, 0), axis=1, keepdims=True)
+        else:
+            split = jnp.sum(jnp.where(single == SPLIT_LANE, row, 0), axis=1, keepdims=True)
+            if one == 0:
+                full = full & (index < split)
+            else:
+                full = full & (index >= split)
+                index = index - split
+        select = onehot((iota((group, CAPS[step]), 1) == index) & full)
+        return source, jnp.dot(
+            select, rings[step][2 * path + one], preferred_element_type=jnp.float32
+        )
+
+    def put(path, source, found):
+        mids[path][source] = found.reshape(SIDE, SLOTS, span).astype(jnp.bfloat16)
+
+    def deliver(step):
+        for path in range(2):
+            if step < STEPS - 1:
+                for one in range(2):
+                    source, found = spread(path, step, one)
+                    put(path, source, found)
+                    pass_on(path, source)
+            else:
+                source, found = spread(path, step, 0)
+                put(path, source, found + spread(path, step, 1)[1])
+                pass_on(path, source)
+
+    def receive(step):
+        for chunk in range(STEPS - step):
+            for path, one in ways:
+                hop(path, one, step, chunk).wait_recv()
+                if chunk < STEPS - step - 1:
+                    hop(path, one, step + 1, chunk).start()
+
+    pl.semaphore_wait(barrier, 2 * (SIDE - 1) + freqs - 1)
+
+    @pl.loop(1, SIDE)
+    def _(k):
+        for path in range(2):
+            label_copy1(path, lax.rem(here[path] + k, SIDE), here[path]).start()
+
+    for chunk in range(STEPS):
+        for path, one in ways:
+            hop(path, one, 0, chunk).start()
+
+    for path in range(2):
+        select = onehot((iota((group, held), 0) == slot_row[path]) & (axis_row[path] == here[path]))
+        put(path, here[path], jnp.dot(select, panels[path], preferred_element_type=jnp.float32))
+        labels_mid[path, pl.ds(here[path], 1)] = labels_own[path, pl.ds(here[path], 1)]
+
+    @pl.loop(1, SIDE)
+    def _(k):
+        for path in range(2):
+            other = lax.rem(here[path] + k, SIDE)
+            label_copy1(path, other, other).wait_recv()
+
+    @pl.loop(1, SIDE)
+    def _(k):
+        label_copy2(lax.rem(y + k, SIDE), y).start()
+
+    labels_in[y] = labels_mid[0]
+
+    receive(0)
+    for path in range(2):
+        pass_on(path, here[path])
+    deliver(0)
+
+    loads[1].wait()
+    for k in range(columns_ref.shape[2]):
+        for r in range(SIDE):
+            tile = jnp.zeros((blocks.shape[2], blocks.shape[3]), jnp.bfloat16)
+            for j in range(columns_ref.shape[0]):
+                tile = jnp.where(columns_ref[j, 0, k] == r, blocks[k, j], tile)
+            dense[0, pl.ds(k * 64, 64), pl.ds(r * 64, 64)] = tile[:, :64]
+            dense[1, pl.ds(k * 64, 64), pl.ds(r * 64, 64)] = tile[:, 64:]
+
+    receive(1)
+    deliver(1)
+
+    @pl.loop(1, SIDE)
+    def _(k):
+        other = lax.rem(y + k, SIDE)
+        label_copy2(other, other).wait_recv()
+
+    slots = SIDE * group
+    named = labels_in[...].reshape(SIDE * SIDE, 128)
+    flags = jnp.where(iota((SIDE * SIDE, 128), 1) == FLAG_LANE, named, 0)
+    flag = jnp.max(jnp.max(flags, axis=1, keepdims=True), axis=0, keepdims=True)
+    flag_ref[...] = jnp.broadcast_to(flag, flag_ref.shape)
+    pick = iota((SIDE * SIDE, SLOTS, 128), 1) + y * SLOTS == iota((SIDE * SIDE, SLOTS, 128), 2)
+    label = jnp.sum(jnp.where(pick, named[:, None, :], 0), axis=2, keepdims=True)
+    label = label.reshape(slots, 1) - 1
+    chosen = onehot(iota((slots, dense.shape[2]), 1) == label)
+    dims = (((1,), (1,)), ((), ()))
+    real = lax.dot_general(chosen, dense[0], dims, preferred_element_type=jnp.float32)
+    imag = lax.dot_general(chosen, dense[1], dims, preferred_element_type=jnp.float32)
+    left[0, :, pl.ds(0, tx)] = real.astype(jnp.bfloat16)
+    left[0, :, pl.ds(tx, tx)] = (-imag).astype(jnp.bfloat16)
+    left[1, :, pl.ds(0, tx)] = imag.astype(jnp.bfloat16)
+    left[1, :, pl.ds(tx, tx)] = real.astype(jnp.bfloat16)
+
+    receive(2)
+    deliver(2)
+    receive(3)
+    deliver(3)
+
+    loads[2].wait()
+
+    @pl.loop(0, SIDE)
+    def _(piece):
+        part, tile = piece // 4, lax.rem(piece, 4)
+        rows = pl.ds(pl.multiple_of(tile * 128, 128), 128)
+        product[part, rows] = jnp.dot(
+            left[part, rows], fields[...], preferred_element_type=jnp.float32
+        )
+
+    def term(part, block, index):
+        rows = pl.ds(pl.multiple_of(index * SLOTS, SLOTS), SLOTS)
+        both = product[part, rows] * block.astype(jnp.float32)
+        return both[:, :cells] + both[:, cells : 2 * cells] + both[:, 2 * cells :]
+
+    total[...] = jnp.zeros_like(total)
+
+    @pl.loop(0, SIDE)
+    def _(source):
+        total[...] += term(0, mid_a[source, y], at(y, source)) - term(
+            1, mid_b[source, z], at(source, z)
+        )
+
+    @pl.loop(0, SIDE)
+    def _(step):
+        source_z, source_y = back(z, SIDE - 1 - step), back(y, SIDE - 1 - step)
+
+        @pl.loop(0, SIDE - 1)
+        def _(inner):
+            column, row = back(y, inner), back(z, inner)
+            index_a, index_b = at(column, source_z), at(source_y, row)
+            second_a(source_z, column, column).wait_recv()
+            second_b(source_y, row, row).wait_recv()
+            total[...] += term(0, in_a[index_a], index_a) - term(1, in_b[index_b], index_b)
+
+    partial[...] = jnp.sum(total[...], axis=0, keepdims=True)
+
+    def sum_copy(other, row):
+        return remote(
+            partial, gathered.at[row], sum_send_sem.at[other], sum_recv_sem.at[row], freq=other
+        )
+
+    @pl.loop(1, freqs)
+    def _(k):
+        sum_copy(lax.rem(mine + k, freqs), mine).start()
+
+    gathered[mine] = partial[...]
+
+    for step in range(STEPS):
+        for chunk in range(STEPS - step):
+            for path, one in ways:
+                hop(path, one, step, chunk).wait_send()
+
+    @pl.loop(1, SIDE)
+    def _(k):
+        other_z, other_y = lax.rem(z + k, SIDE), lax.rem(y + k, SIDE)
+        label_copy1(0, other_z, z).wait_send()
+        label_copy1(1, other_y, y).wait_send()
+        label_copy2(other_y, y).wait_send()
+
+        @pl.loop(0, SIDE)
+        def _(source):
+            second_a(source, other_y, y).wait_send()
+            second_b(source, other_z, z).wait_send()
+
+    @pl.loop(1, freqs)
+    def _(k):
+        other = lax.rem(mine + k, freqs)
+        sum_copy(other, other).wait_recv()
+        sum_copy(other, mine).wait_send()
+
+    result = gathered[0]
+    for row in range(1, freqs):
+        result = result + gathered[row]
+    out_ref[...] = result
+
+
 def on_device(
     forward_fields, adjoint_panels, residual_blocks, residual_columns, panel_brick, panel_receiver
 ):
@@ -321,42 +715,30 @@
     half = (SIDE, SIDE, SLOTS, span)
     any_space = pl.BlockSpec(memory_space=pl.ANY)
     vmem = pl.BlockSpec(memory_space=pltpu.VMEM)
-    summed = pl.pallas_call(
-        functools.partial(kernel, freqs),
-        out_shape=jax.ShapeDtypeStruct((1, cells), jnp.float32),
-        in_specs=[
-            pl.BlockSpec(memory_space=pltpu.SMEM), vmem, vmem, any_space, any_space, any_space,
-        ],
-        out_specs=vmem,
-        scratch_shapes=[
-            pltpu.VMEM((held, 2, span), jnp.bfloat16),
-            pltpu.VMEM((2, held, span), jnp.bfloat16),
-            pltpu.VMEM(fields.shape, jnp.bfloat16),
-            pltpu.VMEM(blocks.shape, jnp.bfloat16),
-            pltpu.VMEM(half, jnp.bfloat16),
-            pltpu.VMEM(half, jnp.bfloat16),
-            pltpu.VMEM(half, jnp.bfloat16),
-            pltpu.VMEM(half, jnp.bfloat16),
-            pltpu.VMEM((bricks, SLOTS, span), jnp.bfloat16),
-            pltpu.VMEM((bricks, SLOTS, span), jnp.bfloat16),
-            pltpu.VMEM((SIDE, 128), jnp.int32),
-            pltpu.VMEM((SIDE, 128), jnp.int32),
-            pltpu.VMEM((SIDE, SIDE, 128), jnp.int32),
-            pltpu.VMEM((2, tx, 512), jnp.bfloat16),
-            pltpu.VMEM((2, slots, 2 * tx), jnp.bfloat16),
-            pltpu.VMEM((2, slots, span), jnp.float32),
-            pltpu.VMEM((SLOTS, cells), jnp.float32),
-            pltpu.VMEM((1, cells), jnp.float32),
-            pltpu.VMEM((freqs, 1, cells), jnp.float32),
-            pltpu.SemaphoreType.DMA((3,)),
-            *[pltpu.SemaphoreType.DMA((SIDE,))] * 8,
-            *[pltpu.SemaphoreType.DMA((bricks,))] * 4,
-            pltpu.SemaphoreType.DMA((freqs,)),
-            pltpu.SemaphoreType.DMA((freqs,)),
-        ],
-        compiler_params=pltpu.CompilerParams(collective_id=0, has_side_effects=True),
-        name="exchange_and_correlate",
-    )(
+    in_specs = [
+        pl.BlockSpec(memory_space=pltpu.SMEM), vmem, vmem, any_space, any_space, any_space,
+    ]
+    loaded = [
+        pltpu.VMEM((held, 2, span), jnp.bfloat16),
+        pltpu.VMEM((2, held, span), jnp.bfloat16),
+        pltpu.VMEM(fields.shape, jnp.bfloat16),
+        pltpu.VMEM(blocks.shape, jnp.bfloat16),
+    ]
+    halves = [pltpu.VMEM(half, jnp.bfloat16)] * 2
+    arrived = [pltpu.VMEM((bricks, SLOTS, span), jnp.bfloat16)] * 2
+    work = [
+        pltpu.VMEM((2, tx, 512), jnp.bfloat16),
+        pltpu.VMEM((2, slots, 2 * tx), jnp.bfloat16),
+        pltpu.VMEM((2, slots, span), jnp.float32),
+        pltpu.VMEM((SLOTS, cells), jnp.float32),
+        pltpu.VMEM((1, cells), jnp.float32),
+        pltpu.VMEM((freqs, 1, cells), jnp.float32),
+    ]
+
+    def dma(*shape):
+        return pltpu.SemaphoreType.DMA(shape)
+
+    args = (
         residual_columns.transpose(2, 0, 1),
         panel_brick.reshape(1, held),
         panel_receiver.reshape(1, held),
@@ -364,6 +746,58 @@
         fields,
         blocks,
     )
+    gradient = jax.ShapeDtypeStruct((1, cells), jnp.float32)
+    summed, flag = pl.pallas_call(
+        functools.partial(compact_kernel, freqs),
+        out_shape=[gradient, jax.ShapeDtypeStruct((1, 128), jnp.int32)],
+        in_specs=in_specs,
+        out_specs=[vmem, vmem],
+        scratch_shapes=[
+            *loaded,
+            pltpu.VMEM((4, CAPS[0], span), jnp.bfloat16),
+            *[pltpu.VMEM((4, cap, span), jnp.bfloat16) for cap in CAPS],
+            *halves,
+            *arrived,
+            pltpu.VMEM((2, SIDE, 128), jnp.int32),
+            pltpu.VMEM((2, SIDE, 128), jnp.int32),
+            pltpu.VMEM((SIDE, SIDE, 128), jnp.int32),
+            *work,
+            dma(3),
+            *[dma(2, SIDE)] * 2,
+            *[dma(SIDE)] * 2,
+            *[dma(4 * STEPS * STEPS)] * 2,
+            *[dma(bricks)] * 4,
+            *[dma(freqs)] * 2,
+        ],
+        compiler_params=pltpu.CompilerParams(collective_id=0, has_side_effects=True),
+        name="compact_exchange",
+    )(*args)
+
+    def padded():
+        return pl.pallas_call(
+            functools.partial(padded_kernel, freqs),
+            out_shape=gradient,
+            in_specs=in_specs,
+            out_specs=vmem,
+            scratch_shapes=[
+                *loaded,
+                *halves,
+                *halves,
+                *arrived,
+                pltpu.VMEM((SIDE, 128), jnp.int32),
+                pltpu.VMEM((SIDE, 128), jnp.int32),
+                pltpu.VMEM((SIDE, SIDE, 128), jnp.int32),
+                *work,
+                dma(3),
+                *[dma(SIDE)] * 8,
+                *[dma(bricks)] * 4,
+                *[dma(freqs)] * 2,
+            ],
+            compiler_params=pltpu.CompilerParams(collective_id=1, has_side_effects=True),
+            name="padded_exchange",
+        )(*args)
+
+    summed = lax.cond(flag[0, 0] > 0, padded, lambda: summed)
     share = cells // freqs
     return lax.dynamic_slice_in_dim(summed[0], lax.axis_index("freq") * share, share, 0)
 

time: 98.9 us -> 86.9 us (0.88)
  Pallas kernels: 97.5 us -> 85.5 us
    pallas_call x1, Pallas kernels: 97.5 us -> 85.5 us  [on_device(): pl.pallas_call(functools.partial(compact_kernel, freqs), out_shape=[gradi...]
where the time goes in v4:
time: 86.9 us; the launch traced here: 86.8 us
  Pallas kernels  85.5 us (98%)
    pallas_call x1, Pallas kernels, on_device(): pl.pallas_call(functools.partial(compact_kernel, freqs), out_shape=[gradi...  85.5 us

profile of v4, /device:TPU:1, one launch (start us, length us, event | category | flops | bytes accessed | tf_op | source)
XLA Modules:
  0.0 86.8 jit_solution(1526191544679915249)
XLA Ops:
  0.0 0.0 copy-start.2
  0.0 0.0 copy-start.3
  0.0 0.0 copy-start.4
  0.0 0.0 copy-start
  0.0 0.0 copy-start.1
  0.0 85.5 %compact_exchange.1 = (f32[1,512]{1,0:T(1,128)S(1)}, s32[1,128]{1,0:T(1,128)}) custom-call(s32[3,1,8]{2,1,0:T(1,128)} %bitcast.16, s32[1,256]{1,0:T(1,128)} %bitcast.18, s32[1,256]{1,0:T(1,128)} %bitcast.20, bf16[256,2,1536]{2,1,0:T(2,128)(2,1)} %bitcast.12, bf16[1024,1536]{1,0:T(8,128)(2,1)} %bitcast.10, bf16[8,3,64,128]{3,2,1,0:T(8,128)(2,1)} %bitcast.14), custom_call_target="tpu_custom_call" | custom-call | tf_op jit(solution)/shard_map/compact_exchange/pallas_call | solution.py:750
  86.1 0.0 copy-done.2
  86.1 0.0 copy-done.3
  86.1 0.0 copy-done.4
  86.1 0.0 copy-done
  86.2 0.0 copy-done.1
  86.2 0.6 dynamic-slice_bitcast_fusion
  (1 shorter events, 0.0 us)
Async XLA Ops:
  0.0 86.1 %copy-start.2 = (s32[1,8,3]{1,0,2:T(1,128)S(1)}, s32[1,8,3]{1,0,2:T(1,128)}, u32[]{:S(2)}) copy-start(s32[1,8,3]{1,0,2:T(1,128)} %param.11) | copy-start | bytes 292
  0.0 86.1 %copy-start.3 = (s32[256,1]{0,1:T(1,128)S(1)}, s32[256,1]{0,1:T(1,128)}, u32[]{:S(2)}) copy-start(s32[256,1]{0,1:T(1,128)} %param.12) | copy-start | bytes 3076
  0.0 86.1 %copy-start.4 = (s32[256]{0:T(256)S(1)}, s32[256]{0:T(256)}, u32[]{:S(2)}) copy-start(s32[256]{0:T(256)} %param.13) | copy-start | bytes 3076
  0.0 86.1 %copy-start = (bf16[1,1,2,512,1536]{4,3,2,1,0:T(8,128)(2,1)S(1)}, bf16[1,1,2,512,1536]{4,3,2,1,0:T(8,128)(2,1)}, u32[]{:S(2)}) copy-start(bf16[1,1,2,512,1536]{4,3,2,1,0:T(8,128)(2,1)} %param.8) | copy-start | bytes 9437188
  0.0 86.1 %copy-start.1 = (bf16[1,1,8,3,64,128]{5,4,3,2,1,0:T(8,128)(2,1)S(1)}, bf16[1,1,8,3,64,128]{5,4,3,2,1,0:T(8,128)(2,1)}, u32[]{:S(2)}) copy-start(bf16[1,1,8,3,64,128]{5,4,3,2,1,0:T(8,128)(2,1)} %param.10) | copy-start | bytes 1179652

commit v5 on v4

--- a/solution.py
+++ b/solution.py
@@ -10,8 +10,8 @@
 SIDE = 8
 SLOTS = 8
 MESH = pl.DeviceIdType.MESH
-CAPS = (128, 112, 80, 48)
-EDGES = (0, 48, 80, 112, 128)
+CAPS = (128, 104, 72, 40)
+EDGES = (0, 40, 72, 104, 128)
 STEPS = len(CAPS)
 START_LANE, SPLIT_LANE, FLAG_LANE = 64, 65, 127
 
@@ -446,9 +446,9 @@
         over = jnp.maximum(over, too_long)
         for one in range(2):
             select = onehot((iota((CAPS[0], held), 0) == place) & (list_row == one))
-            lists[2 * path + one] = jnp.dot(
-                select, panels[path], preferred_element_type=jnp.float32
-            ).astype(jnp.bfloat16)
+            found = jnp.dot(select, panels[path], preferred_element_type=jnp.float32)
+            found = found.reshape(CAPS[0] // SLOTS, SLOTS, span)
+            lists[2 * path + one] = found.astype(jnp.bfloat16)
         names = iota((SIDE, held), 0) == axis_row[path]
         by_lane = onehot(slot_col[path] == iota((held, 128), 1))
         high = jnp.where(names, value // 16, 0).astype(jnp.float32).astype(jnp.bfloat16)
@@ -476,7 +476,7 @@
 
     def hop(path, one, step, chunk):
         part = 2 * path + one
-        piece = pl.ds(EDGES[chunk], EDGES[chunk + 1] - EDGES[chunk])
+        piece = pl.ds(EDGES[chunk] // SLOTS, (EDGES[chunk + 1] - EDGES[chunk]) // SLOTS)
         source = lists if step == 0 else rings[step - 1]
         index = (part * STEPS + step) * STEPS + chunk
         other = lax.rem(here[path] + (1 if one == 0 else SIDE - 1), SIDE)
@@ -527,8 +527,9 @@
                 full = full & (index >= split)
                 index = index - split
         select = onehot((iota((group, CAPS[step]), 1) == index) & full)
+        rows = rings[step][2 * path + one].astype(jnp.float32).reshape(CAPS[step], span)
         return source, jnp.dot(
-            select, rings[step][2 * path + one], preferred_element_type=jnp.float32
+            select, rows.astype(jnp.bfloat16), preferred_element_type=jnp.float32
         )
 
     def put(path, source, found):
@@ -754,8 +755,8 @@
         out_specs=[vmem, vmem],
         scratch_shapes=[
             *loaded,
-            pltpu.VMEM((4, CAPS[0], span), jnp.bfloat16),
-            *[pltpu.VMEM((4, cap, span), jnp.bfloat16) for cap in CAPS],
+            pltpu.VMEM((4, CAPS[0] // SLOTS, SLOTS, span), jnp.bfloat16),
+            *[pltpu.VMEM((4, cap // SLOTS, SLOTS, span), jnp.bfloat16) for cap in CAPS],
             *halves,
             *arrived,
             pltpu.VMEM((2, SIDE, 128), jnp.int32),

time: 86.9 us -> 85.3 us (0.982)
  Pallas kernels: 85.5 us -> 83.9 us
    pallas_call x1, Pallas kernels: 85.5 us -> 83.9 us  [on_device(): pl.pallas_call(functools.partial(compact_kernel, freqs), out_shape=[gradi...]
where the time goes in v5:
time: 85.3 us; the launch traced here: 85.2 us
  Pallas kernels  83.9 us (98%)
    pallas_call x1, Pallas kernels, on_device(): pl.pallas_call(functools.partial(compact_kernel, freqs), out_shape=[gradi...  83.9 us

profile of v5, /device:TPU:1, one launch (start us, length us, event | category | flops | bytes accessed | tf_op | source)
XLA Modules:
  0.0 85.2 jit_solution(13032825587687063320)
XLA Ops:
  0.0 0.0 copy-start.2
  0.0 0.0 copy-start.3
  0.0 0.0 copy-start.4
  0.0 0.0 copy-start
  0.0 0.0 copy-start.1
  0.0 83.9 %compact_exchange.1 = (f32[1,512]{1,0:T(1,128)S(1)}, s32[1,128]{1,0:T(1,128)}) custom-call(s32[3,1,8]{2,1,0:T(1,128)} %bitcast.16, s32[1,256]{1,0:T(1,128)} %bitcast.18, s32[1,256]{1,0:T(1,128)} %bitcast.20, bf16[256,2,1536]{2,1,0:T(2,128)(2,1)} %bitcast.12, bf16[1024,1536]{1,0:T(8,128)(2,1)} %bitcast.10, bf16[8,3,64,128]{3,2,1,0:T(8,128)(2,1)} %bitcast.14), custom_call_target="tpu_custom_call" | custom-call | tf_op jit(solution)/shard_map/compact_exchange/pallas_call | solution.py:751
  84.5 0.0 copy-done.2
  84.5 0.0 copy-done.3
  84.6 0.0 copy-done.4
  84.6 0.0 copy-done
  84.6 0.0 copy-done.1
  84.6 0.6 dynamic-slice_bitcast_fusion
  (1 shorter events, 0.0 us)
Async XLA Ops:
  0.0 84.5 %copy-start.2 = (s32[1,8,3]{1,0,2:T(1,128)S(1)}, s32[1,8,3]{1,0,2:T(1,128)}, u32[]{:S(2)}) copy-start(s32[1,8,3]{1,0,2:T(1,128)} %param.11) | copy-start | bytes 292
  0.0 84.5 %copy-start.3 = (s32[256,1]{0,1:T(1,128)S(1)}, s32[256,1]{0,1:T(1,128)}, u32[]{:S(2)}) copy-start(s32[256,1]{0,1:T(1,128)} %param.12) | copy-start | bytes 3076
  0.0 84.6 %copy-start.4 = (s32[256]{0:T(256)S(1)}, s32[256]{0:T(256)}, u32[]{:S(2)}) copy-start(s32[256]{0:T(256)} %param.13) | copy-start | bytes 3076
  0.0 84.6 %copy-start = (bf16[1,1,2,512,1536]{4,3,2,1,0:T(8,128)(2,1)S(1)}, bf16[1,1,2,512,1536]{4,3,2,1,0:T(8,128)(2,1)}, u32[]{:S(2)}) copy-start(bf16[1,1,2,512,1536]{4,3,2,1,0:T(8,128)(2,1)} %param.8) | copy-start | bytes 9437188
  0.0 84.6 %copy-start.1 = (bf16[1,1,8,3,64,128]{5,4,3,2,1,0:T(8,128)(2,1)S(1)}, bf16[1,1,8,3,64,128]{5,4,3,2,1,0:T(8,128)(2,1)}, u32[]{:S(2)}) copy-start(bf16[1,1,8,3,64,128]{5,4,3,2,1,0:T(8,128)(2,1)} %param.10) | copy-start | bytes 1179652

commit v6 on v5

--- a/solution.py
+++ b/solution.py
@@ -536,13 +536,14 @@
         mids[path][source] = found.reshape(SIDE, SLOTS, span).astype(jnp.bfloat16)
 
     def deliver(step):
-        for path in range(2):
-            if step < STEPS - 1:
-                for one in range(2):
+        if step < STEPS - 1:
+            for one in range(2):
+                for path in range(2):
                     source, found = spread(path, step, one)
                     put(path, source, found)
                     pass_on(path, source)
-            else:
+        else:
+            for path in range(2):
                 source, found = spread(path, step, 0)
                 put(path, source, found + spread(path, step, 1)[1])
                 pass_on(path, source)

time: 85.3 us -> 85.3 us (level)
  no operation moved by 1% of the time
where the time goes in v6:
time: 85.3 us; the launch traced here: 85.2 us
  Pallas kernels  83.9 us (98%)
    pallas_call x1, Pallas kernels, on_device(): pl.pallas_call(functools.partial(compact_kernel, freqs), out_shape=[gradi...  83.9 us

profile of v6, /device:TPU:1, one launch (start us, length us, event | category | flops | bytes accessed | tf_op | source)
XLA Modules:
  0.0 85.2 jit_solution(6181921938617040838)
XLA Ops:
  0.0 0.0 copy-start.2
  0.0 0.0 copy-start.3
  0.0 0.0 copy-start.4
  0.0 0.0 copy-start
  0.0 0.0 copy-start.1
  0.0 83.9 %compact_exchange.1 = (f32[1,512]{1,0:T(1,128)S(1)}, s32[1,128]{1,0:T(1,128)}) custom-call(s32[3,1,8]{2,1,0:T(1,128)} %bitcast.16, s32[1,256]{1,0:T(1,128)} %bitcast.18, s32[1,256]{1,0:T(1,128)} %bitcast.20, bf16[256,2,1536]{2,1,0:T(2,128)(2,1)} %bitcast.12, bf16[1024,1536]{1,0:T(8,128)(2,1)} %bitcast.10, bf16[8,3,64,128]{3,2,1,0:T(8,128)(2,1)} %bitcast.14), custom_call_target="tpu_custom_call" | custom-call | tf_op jit(solution)/shard_map/compact_exchange/pallas_call | solution.py:752
  84.5 0.0 copy-done.2
  84.5 0.0 copy-done.3
  84.6 0.0 copy-done.4
  84.6 0.0 copy-done
  84.6 0.0 copy-done.1
  84.6 0.6 dynamic-slice_bitcast_fusion
  (1 shorter events, 0.0 us)
Async XLA Ops:
  0.0 84.5 %copy-start.2 = (s32[1,8,3]{1,0,2:T(1,128)S(1)}, s32[1,8,3]{1,0,2:T(1,128)}, u32[]{:S(2)}) copy-start(s32[1,8,3]{1,0,2:T(1,128)} %param.11) | copy-start | bytes 292
  0.0 84.5 %copy-start.3 = (s32[256,1]{0,1:T(1,128)S(1)}, s32[256,1]{0,1:T(1,128)}, u32[]{:S(2)}) copy-start(s32[256,1]{0,1:T(1,128)} %param.12) | copy-start | bytes 3076
  0.0 84.6 %copy-start.4 = (s32[256]{0:T(256)S(1)}, s32[256]{0:T(256)}, u32[]{:S(2)}) copy-start(s32[256]{0:T(256)} %param.13) | copy-start | bytes 3076
  0.0 84.6 %copy-start = (bf16[1,1,2,512,1536]{4,3,2,1,0:T(8,128)(2,1)S(1)}, bf16[1,1,2,512,1536]{4,3,2,1,0:T(8,128)(2,1)}, u32[]{:S(2)}) copy-start(bf16[1,1,2,512,1536]{4,3,2,1,0:T(8,128)(2,1)} %param.8) | copy-start | bytes 9437188
  0.0 84.6 %copy-start.1 = (bf16[1,1,8,3,64,128]{5,4,3,2,1,0:T(8,128)(2,1)S(1)}, bf16[1,1,8,3,64,128]{5,4,3,2,1,0:T(8,128)(2,1)}, u32[]{:S(2)}) copy-start(bf16[1,1,8,3,64,128]{5,4,3,2,1,0:T(8,128)(2,1)} %param.10) | copy-start | bytes 1179652
